TPU v7x, 512 devices: a whole 4x8x8 slice. The times are simulated.
512 devices in a mesh: tm: 4 (over y_hi, core), pix: 128 (over x, z, y_lo).
Axes of the slice: x: 4, y: 8 (y_hi: 2, y_lo: 4; y = y_hi * 4 + y_lo), z: 8, core: 2. Of those that a mesh axis runs over, the one named last changes fastest.
Arguments:
- activations: bfloat16 [4, 327680, 256], P('tm', 'pix'), may hold values from -6 to 6
- down_weight: bfloat16 [1024, 256], replicated, may hold values from -0.1875 to 0.1875
- down_bias: float32 [256], replicated, may hold values from -3 to 3
- taps: float32 [9, 256], replicated, may hold values from -2 to 2
- point_weight: bfloat16 [256, 256], replicated, may hold values from -0.375 to 0.375
- time_mix: float32 [4, 4, 256], replicated, may hold values from -3 to 3
- edge_rows: int32 [128, 2, 20], P('pix'), may hold values from 0 to 19, as said below
- cotangent: bfloat16 [4, 81920, 256], P(None, ('pix', 'tm')), may hold values from -6 to 6
Outputs:
- grad_input: bfloat16 [4, 327680, 256], P('tm', 'pix')
- grad_down: float32 [1024, 256], replicated
- grad_bias: float32 [256], replicated
- grad_taps: float32 [9, 256], replicated
- grad_point: float32 [256, 256], replicated
- grad_mix: float32 [4, 4, 256], replicated
Inputs may be any that keep to these rules, and one draw needn't show every extreme that they name: Each edge_rows[t, e] is either 0, 1, .., 19 or its reversal; edge_rows[t, 1] equals edge_rows[(t + 1) mod 128, 0].
All inputs are finite; a program needn't handle non-finite values.
Results may differ from a plain program's by a relative error of at most 0.014.
Values may be sent and summed in bfloat16 or wider, within the bound.
No kernel may reach another device: no remote copies, remote signals or barrier semaphores. Data moves between devices by JAX's collectives and lax.ppermute only.
A program may use at most 64 MiB of HBM per device.

v0:
```python
import math
import jax
import jax.numpy as jnp
from jax import lax
from jax.sharding import PartitionSpec as P

C = 256
TR = 20
TC = 32


def padded_2(cells, sides, width):
    for axis, dim in sides:
        count = lax.axis_size(axis)
        head = lax.slice_in_dim(cells, 0, width, axis=dim)
        tail = lax.slice_in_dim(cells, cells.shape[dim] - width, cells.shape[dim], axis=dim)
        cells = jnp.concatenate(
            [
                lax.ppermute(tail, axis, [(i, (i + 1) % count) for i in range(count)]),
                cells,
                lax.ppermute(head, axis, [((i + 1) % count, i) for i in range(count)]),
            ],
            axis=dim,
        )
    return cells


def on_device(
    activations, down_weight, down_bias, taps, point_weight, time_mix, edge_rows, cotangent
):
    frames = lax.axis_size("tm")
    tiles = lax.axis_size("pix")
    pixels = TR * TC
    scale = 1.0 / math.sqrt(frames * tiles * pixels)
    rows_in = activations.reshape(pixels, 4 * C)
    preact = jnp.dot(rows_in, down_weight, preferred_element_type=jnp.float32) + down_bias
    pooled = jax.nn.silu(preact).astype(jnp.bfloat16)
    tile_grid = pooled.reshape(1, TR, TC, C)
    padded = padded_2(tile_grid, (("pix", 2),), 1)
    west_map = edge_rows[0, 0]
    east_map = edge_rows[0, 1]
    west_col = jnp.take(padded[0, :, 0, :], west_map, axis=0)
    east_col = jnp.take(padded[0, :, TC + 1, :], east_map, axis=0)
    widened = jnp.concatenate([west_col[:, None, :], tile_grid[0], east_col[:, None, :]], axis=1)
    widened = jnp.pad(widened, ((1, 1), (0, 0), (0, 0)))
    spread = jnp.zeros((TR, TC, C), jnp.float32)
    for row_off in range(3):
        for col_off in range(3):
            spread = (
                spread
                + taps[row_off * 3 + col_off]
                * widened[row_off : row_off + TR, col_off : col_off + TC, :]
            )
    spread_low = spread.astype(jnp.bfloat16).reshape(pixels, C)
    mixed_in = (
        pooled.astype(jnp.float32)
        + jnp.dot(spread_low, point_weight, preferred_element_type=jnp.float32)
    ).astype(jnp.bfloat16)
    by_pixel = lax.all_to_all(
        mixed_in.reshape(1, pixels, C), "tm", split_axis=1, concat_axis=0, tiled=True
    )
    mix_part = jnp.einsum("gpc,fpc->fgc", by_pixel, cotangent, preferred_element_type=jnp.float32)
    cot_f = cotangent.astype(jnp.float32)
    mixed_acc = jnp.zeros((frames, cotangent.shape[1], C), jnp.float32)
    for source in range(frames):
        mixed_acc = mixed_acc + time_mix[source][:, None, :] * cot_f[source][None, :, :]
    mixed_grad = mixed_acc.astype(jnp.bfloat16)
    back_grad = lax.all_to_all(mixed_grad, "tm", split_axis=0, concat_axis=1, tiled=True)
    mixed_rows = back_grad.reshape(pixels, C)
    point_part = jnp.dot(spread_low.T, mixed_rows, preferred_element_type=jnp.float32)
    spread_grad = jnp.dot(mixed_rows, point_weight.T, preferred_element_type=jnp.float32).astype(
        jnp.bfloat16
    )
    grad_float = spread_grad.reshape(TR, TC, C).astype(jnp.float32)
    taps_rows = []
    for row_off in range(3):
        for col_off in range(3):
            taps_rows.append(
                jnp.sum(
                    grad_float * widened[row_off : row_off + TR, col_off : col_off + TC, :],
                    axis=(0, 1),
                )
            )
    taps_part = jnp.stack(taps_rows, axis=0)
    grad_padded = jnp.pad(grad_float, ((2, 2), (2, 2), (0, 0)))
    wide_grad = jnp.zeros((TR + 2, TC + 2, C), jnp.float32)
    for row_off in range(3):
        for col_off in range(3):
            wide_grad = (
                wide_grad
                + taps[row_off * 3 + col_off]
                * grad_padded[2 - row_off : 4 - row_off + TR, 2 - col_off : 4 - col_off + TC, :]
            )
    west_back = jnp.take(wide_grad[1 : TR + 1, 0, :], west_map, axis=0)
    east_back = jnp.take(wide_grad[1 : TR + 1, TC + 1, :], east_map, axis=0)
    outgoing = jnp.stack([west_back, east_back], axis=1)
    incoming = padded_2(outgoing.astype(jnp.bfloat16), (("pix", 1),), 1).astype(outgoing.dtype)
    inner_grad = wide_grad[1 : TR + 1, 1 : TC + 1, :]
    inner_grad = inner_grad.at[:, 0, :].add(incoming[:, 0, :])
    inner_grad = inner_grad.at[:, TC - 1, :].add(incoming[:, 3, :])
    pooled_grad = mixed_rows.astype(jnp.float32) + inner_grad.reshape(pixels, C)
    sigma = jax.nn.sigmoid(preact)
    pre_grad = (pooled_grad * (sigma * (1.0 + preact * (1.0 - sigma)))).astype(jnp.bfloat16)
    bias_part = jnp.sum(pre_grad.astype(jnp.float32), axis=0)
    down_part = jnp.dot(rows_in.T, pre_grad, preferred_element_type=jnp.float32)
    grad_input = jnp.dot(pre_grad, down_weight.T, preferred_element_type=jnp.float32).astype(
        jnp.bfloat16
    )
    terms = (
        down_part,
        point_part,
        taps_part,
        mix_part.reshape(frames * frames, C),
        bias_part.reshape(1, C),
    )
    totals = lax.psum((terms[0], terms[1], terms[2], terms[3], terms[4]), ("tm", "pix"))
    grad_down = totals[0] * scale
    grad_point = totals[1] * scale
    grad_taps = totals[2] * scale
    grad_mix = totals[3].reshape(frames, frames, C) * scale
    grad_bias = totals[4].reshape(C) * scale
    return (
        grad_input.reshape(1, 4 * pixels, C),
        grad_down,
        grad_bias,
        grad_taps,
        grad_point,
        grad_mix,
    )


def solution(mesh):
    in_specs = (
        P("tm", "pix", None),
        P(),
        P(),
        P(),
        P(),
        P(),
        P("pix", None, None),
        P(None, ("pix", "tm"), None),
    )
    out_specs = (P("tm", "pix", None), P(), P(), P(), P(), P())
    return jax.shard_map(
        on_device, mesh=mesh, in_specs=in_specs, out_specs=out_specs, check_vma=False
    )
```

profile of v0, /device:TPU:24, one launch (start us, length us, event | category | flops | bytes accessed | tf_op | source)
XLA Modules:
  0.0 374.9 jit_solution(8974585061847904464)
XLA Ops:
  7.2 0.0 copy-start
  7.2 0.8 slice_bitcast_fusion.9
  8.0 1.0 convert_element_type.87
  9.0 0.0 copy-start.7
  9.0 0.0 copy-start.6
  9.0 0.0 copy-start.3
  9.1 0.9 add_convert_fusion
  10.0 4.4 %all-to-all-start = ((bf16[4,160,256]{2,1,0:T(8,128)(2,1)}), bf16[4,160,256]{2,1,0:T(8,128)(2,1)S(1)}, u32[]{:S(2)}, u32[]{:S(2)}) async-start(bf16[4,160,256]{2,1,0:T(8,128)(2,1)} %add_convert_fusion), calls=%async_computation | async-start | bytes 655360 | tf_op jit(solution)/shard_map/all_to_all | solution.py:68
  14.5 10.7 %all-to-all-done = bf16[4,160,256]{2,1,0:T(8,128)(2,1)S(1)} async-done(((bf16[4,160,256]{2,1,0:T(8,128)(2,1)}), bf16[4,160,256]{2,1,0:T(8,128)(2,1)S(1)}, u32[]{:S(2)}, u32[]{:S(2)}) %all-to-all-start) | async-done | bytes 327712 | tf_op jit(solution)/shard_map/all_to_all | solution.py:68
  25.1 0.3 fusion.1
  25.4 0.4 copy.50
  25.8 0.0 copy-start.2
  25.8 0.6 fusion.12
  26.4 0.0 copy-start.1
  26.4 0.9 copy-done.1
  27.3 0.6 gather_fusion.1
  27.9 0.1 fusion.49
  28.0 6.7 %collective-permute-start.1 = (bf16[20,1,256]{2,0,1:T(8,128)(2,1)S(1)}, bf16[20,1,256]{2,0,1:T(8,128)(2,1)S(1)}, u32[]{:S(2)}, u32[]{:S(2)}) collective-permute-start(bf16[20,1,256]{2,0,1:T(8,128)(2,1)S(1)} %fusion.49), channel_id=1, source_target_pairs={{1,0},{2,1},{3,2},{4,3},{5,4},{6,5},{7,6},{8,7},{9,8},{10,9},{11,1... | collective-permute-start | bytes 30728 | tf_op jit(solution)/shard_map/ppermute | solution.py:21
  34.7 0.6 gather_fusion
  35.3 0.1 fusion.48
  35.4 1.9 collective-permute-start
  37.3 1.1 copy.60
  38.4 2.5 reshape.139
  40.9 0.0 copy-start.8
  40.9 1.2 slice.257
  42.1 0.0 collective-permute-done.1
  42.1 0.7 fusion.47
  42.9 0.2 copy.51
  43.1 0.8 fusion.34
  43.9 1.6 convolution_bitcast_fusion
  45.5 3.9 %collective-permute-start.3 = (bf16[1,20,1,256]{3,1,2,0:T(8,128)(2,1)S(1)}, bf16[1,20,1,256]{3,1,2,0:T(8,128)(2,1)S(1)}, u32[]{:S(2)}, u32[]{:S(2)}) collective-permute-start(bf16[1,20,1,256]{3,1,2,0:T(8,128)(2,1)S(1)} %copy.65), channel_id=1, source_target_pairs={{1,0},{2,1},{3,2},{4,3},{5,4},{6,5},{7,6},{8,7},{9,8},{10,9},{11,1... | collective-permute-start | bytes 30728 | tf_op jit(solution)/shard_map/ppermute | solution.py:21
  49.4 4.6 %collective-permute-start.2 = (bf16[1,20,1,256]{3,1,2,0:T(8,128)(2,1)S(1)}, bf16[1,20,1,256]{3,1,2,0:T(8,128)(2,1)S(1)}, u32[]{:S(2)}, u32[]{:S(2)}) collective-permute-start(bf16[1,20,1,256]{3,1,2,0:T(8,128)(2,1)S(1)} %copy.64), channel_id=1, source_target_pairs={{0,1},{1,2},{2,3},{3,4},{4,5},{5,6},{6,7},{7,8},{8,9},{9,10},{10,1... | collective-permute-start | bytes 30728 | tf_op jit(solution)/shard_map/ppermute | solution.py:19
  54.1 0.5 convolution_convert_fusion
  54.6 1.6 reshape.140
  56.3 0.6 gather_fusion.3
  56.9 1.8 collective-permute-done.2
  58.6 0.6 gather_fusion.2
  59.2 0.1 select_bitcast_fusion
  59.4 0.2 fusion.45
  59.6 0.8 fusion.30
  60.3 0.2 fusion.2
  60.6 0.5 copy.67
  61.1 0.5 broadcast.135
  61.6 3.4 reduce.5
  65.0 1.8 reshape.191
  66.8 3.5 all-to-all-start.1
  70.2 0.0 all-reduce.6.cloned.1.call-start
  70.3 1.0 fusion.53
  71.3 0.0 all-reduce.6.cloned.1.call-update
  71.3 0.7 fusion.38
  72.1 8.8 %all-to-all-done.1 = bf16[4,2,20480]{2,1,0:T(2,128)(2,1)S(1)} async-done(((bf16[4,2,20480]{2,1,0:T(2,128)(2,1)}), bf16[4,2,20480]{2,1,0:T(2,128)(2,1)S(1)}, u32[]{:S(2)}, u32[]{:S(2)}) %all-to-all-start.1) | async-done | bytes 327712 | tf_op jit(solution)/shard_map/all_to_all | solution.py:59
  80.9 0.3 reshape.192
  81.2 0.1 copy.63
  81.3 0.3 copy.59
  81.6 0.4 convolution_bitcast_fusion.1
  82.0 0.2 copy.61
  82.2 108.8 %all-reduce.2 = (f32[1,256]{1,0:T(1,128)S(1)}, f32[9,256]{1,0:T(8,128)S(1)}, f32[16,256]{1,0:T(8,128)S(1)}) all-reduce(f32[1,256]{1,0:T(1,128)S(1)} %bitcast.136, f32[9,256]{1,0:T(8,128)S(1)} %stack.51, f32[16,256]{1,0:T(8,128)S(1)} %reshape.145), channel_id=1, replica_groups=mesh['tm'=4,'pix'=128] {'tm','pix'}, use_global_device_ids=true, to_apply=%region_2.4 | all-reduce | flops 6656 | bytes 53248 | tf_op jit(solution)/shard_map/psum | solution.py:116
  191.0 0.6 mul.396
  191.6 0.6 broadcast_multiply_fusion.4
  192.2 0.6 broadcast_multiply_fusion.3
  192.8 171.9 %all-reduce.6.cloned.1.call-done = (f32[1024,256]{0,1:T(8,128)}, f32[256,256]{1,0:T(8,128)}) async-done(((f32[1024,256]{0,1:T(8,128)}, f32[256,256]{1,0:T(8,128)}), (f32[1024,256]{0,1:T(8,128)}, f32[256,256]{1,0:T(8,128)})) %all-reduce.6.cloned.1.call-update) | async-done | bytes 1310736 | tf_op jit(solution)/shard_map/psum | solution.py:116
  364.6 1.3 broadcast_multiply_fusion
  366.0 1.3 copy.62
  367.3 0.7 broadcast_multiply_fusion.1
  (27 shorter events, 0.3 us)
Async XLA Ops:
  7.2 35.9 %copy-start = (bf16[1024,256]{1,0:T(8,128)(2,1)S(1)}, bf16[1024,256]{1,0:T(8,128)(2,1)}, u32[]{:S(2)}) copy-start(bf16[1024,256]{1,0:T(8,128)(2,1)} %param.17) | copy-start | bytes 1572868
  9.0 5.4 %copy-start.7 = (s32[1,2,20]{2,1,0:T(2,128)S(1)}, s32[1,2,20]{2,1,0:T(2,128)}, u32[]{:S(2)}) copy-start(s32[1,2,20]{2,1,0:T(2,128)} %param.22) | copy-start | bytes 484
  9.0 5.4 %copy-start.6 = (f32[9,256]{1,0:T(8,128)S(1)}, f32[9,256]{1,0:T(8,128)}, u32[]{:S(2)}) copy-start(f32[9,256]{1,0:T(8,128)} %param.19) | copy-start | bytes 27652
  9.0 16.1 %copy-start.3 = (bf16[256,256]{1,0:T(8,128)(2,1)S(1)}, bf16[256,256]{1,0:T(8,128)(2,1)}, u32[]{:S(2)}) copy-start(bf16[256,256]{1,0:T(8,128)(2,1)} %param.20) | copy-start | bytes 393220
  10.0 15.1 %all-to-all-start = ((bf16[4,160,256]{2,1,0:T(8,128)(2,1)}), bf16[4,160,256]{2,1,0:T(8,128)(2,1)S(1)}, u32[]{:S(2)}, u32[]{:S(2)}) async-start(bf16[4,160,256]{2,1,0:T(8,128)(2,1)} %add_convert_fusion), calls=%async_computation | async-start | bytes 655360 | tf_op jit(solution)/shard_map/all_to_all | solution.py:68
  25.8 11.5 %copy-start.2 = (bf16[4,160,256]{2,1,0:T(8,128)(2,1)S(1)}, bf16[4,160,256]{2,1,0:T(8,128)(2,1)}, u32[]{:S(2)}) copy-start(bf16[4,160,256]{2,1,0:T(8,128)(2,1)} %param.23) | copy-start | bytes 983044
  26.4 0.9 copy-start.1
  28.0 14.1 %collective-permute-start.1 = (bf16[20,1,256]{2,0,1:T(8,128)(2,1)S(1)}, bf16[20,1,256]{2,0,1:T(8,128)(2,1)S(1)}, u32[]{:S(2)}, u32[]{:S(2)}) collective-permute-start(bf16[20,1,256]{2,0,1:T(8,128)(2,1)S(1)} %fusion.49), channel_id=1, source_target_pairs={{1,0},{2,1},{3,2},{4,3},{5,4},{6,5},{7,6},{8,7},{9,8},{10,9},{11,1... | collective-permute-start | bytes 30728 | tf_op jit(solution)/shard_map/ppermute | solution.py:21
  35.4 6.7 %collective-permute-start = (bf16[20,1,256]{2,0,1:T(8,128)(2,1)S(1)}, bf16[20,1,256]{2,0,1:T(8,128)(2,1)S(1)}, u32[]{:S(2)}, u32[]{:S(2)}) collective-permute-start(bf16[20,1,256]{2,0,1:T(8,128)(2,1)S(1)} %fusion.48), channel_id=1, source_target_pairs={{0,1},{1,2},{2,3},{3,4},{4,5},{5,6},{6,7},{7,8},{8,9},{9,10},{10,1... | collective-permute-start | bytes 30728 | tf_op jit(solution)/shard_map/ppermute | solution.py:19
  40.9 2.2 copy-start.8
  45.5 10.7 %collective-permute-start.3 = (bf16[1,20,1,256]{3,1,2,0:T(8,128)(2,1)S(1)}, bf16[1,20,1,256]{3,1,2,0:T(8,128)(2,1)S(1)}, u32[]{:S(2)}, u32[]{:S(2)}) collective-permute-start(bf16[1,20,1,256]{3,1,2,0:T(8,128)(2,1)S(1)} %copy.65), channel_id=1, source_target_pairs={{1,0},{2,1},{3,2},{4,3},{5,4},{6,5},{7,6},{8,7},{9,8},{10,9},{11,1... | collective-permute-start | bytes 30728 | tf_op jit(solution)/shard_map/ppermute | solution.py:21
  49.4 9.2 %collective-permute-start.2 = (bf16[1,20,1,256]{3,1,2,0:T(8,128)(2,1)S(1)}, bf16[1,20,1,256]{3,1,2,0:T(8,128)(2,1)S(1)}, u32[]{:S(2)}, u32[]{:S(2)}) collective-permute-start(bf16[1,20,1,256]{3,1,2,0:T(8,128)(2,1)S(1)} %copy.64), channel_id=1, source_target_pairs={{0,1},{1,2},{2,3},{3,4},{4,5},{5,6},{6,7},{7,8},{8,9},{9,10},{10,1... | collective-permute-start | bytes 30728 | tf_op jit(solution)/shard_map/ppermute | solution.py:19
  66.8 14.1 %all-to-all-start.1 = ((bf16[4,2,20480]{2,1,0:T(2,128)(2,1)}), bf16[4,2,20480]{2,1,0:T(2,128)(2,1)S(1)}, u32[]{:S(2)}, u32[]{:S(2)}) async-start(bf16[4,2,20480]{2,1,0:T(2,128)(2,1)} %reshape.191), calls=%async_computation.1 | async-start | bytes 655360 | tf_op jit(solution)/shard_map/all_to_all | solution.py:59
  70.2 294.4 %all-reduce.6.cloned.1.call-start = ((), (), s32[]{:S(2)}) async-start(), calls=%async_computation.2 | async-start | bytes 2621440 | tf_op jit(solution)/shard_map/psum | solution.py:116
  72.1 9.5 %copy-start.4 = (bf16[4,160,256]{1,0,2:T(4,128)(2,1)S(1)}, bf16[4,160,256]{1,0,2:T(4,128)(2,1)}, u32[]{:S(2)}) copy-start(bf16[4,160,256]{1,0,2:T(4,128)(2,1)} %copy.60) | copy-start | bytes 983044
  366.0 1.3 copy-start.5
Sparse Core Ops, SparseCore 0:
  76.7 287.8 all-reduce.5
where the time goes:
time: 376 us; the launch traced here: 375 us
  waiting for transfers between devices  193 us (51%)
  blocking collectives  109 us (29%)
  starting transfers between devices  25 us (7%)
  local copies, waits for them, and re-layouts  17 us (5%)
  between operations  14.4 us (4%)
  other arithmetic  11.8 us (3%)
  matrix products  4.79 us (1%)
    psum x1, waiting for transfers between devices, on_device(): lax.psum((terms[0], terms[1], terms[2], terms[3], terms[4]), ('tm', 'pix'))  172 us
    psum x1, blocking collectives, on_device(): lax.psum((terms[0], terms[1], terms[2], terms[3], terms[4]), ('tm', 'pix'))  109 us
    all_to_all x1, waiting for transfers between devices, on_device(): lax.all_to_all(mixed_grad, 'tm', split_axis=0, concat_axis=1, tiled=True)  10.7 us
    ppermute x2, starting transfers between devices, padded_2(): lax.ppermute(head, axis, [((i + 1) % count, i) for i in range(count)])  10.6 us
    all_to_all x1, waiting for transfers between devices, on_device(): lax.all_to_all(mixed_in.reshape(1, pixels, C), 'tm', split_axis=1, concat...  8.76 us
  transfers between devices with their start and end apart: 7, of which 4 were waited for; matrix products, arithmetic and copies ran while one was open for 4% of the time, Pallas kernels for 0%

commit v1 on v0

--- a/solution.py
+++ b/solution.py
@@ -113,7 +113,7 @@
         mix_part.reshape(frames * frames, C),
         bias_part.reshape(1, C),
     )
-    totals = lax.psum((terms[0], terms[1], terms[2], terms[3], terms[4]), ("tm", "pix"))
+    totals = lax.psum(lax.psum((terms[0], terms[1], terms[2], terms[3], terms[4]), "pix"), "tm")
     grad_down = totals[0] * scale
     grad_point = totals[1] * scale
     grad_taps = totals[2] * scale

time: 376 us -> 2170 us (5.77)
  the two profiles are of different devices: /device:TPU:24 before, /device:TPU:1 now
where the time goes in v1:
time: 2170 us
  waiting for transfers between devices  1270 us (59%)
  blocking collectives  815 us (38%)
  starting transfers between devices  37.1 us (2%)
    psum x1, waiting for transfers between devices, on_device(): lax.psum((terms[0], terms[1], terms[2], terms[3], terms[4]), 'pix')  1250 us
    psum x1, blocking collectives, on_device(): lax.psum((terms[0], terms[1], terms[2], terms[3], terms[4]), 'pix')  618 us
    psum x1, blocking collectives, on_device(): lax.psum(lax.psum((terms[0], terms[1], terms[2], terms[3], terms[4]), 'pi...  197 us
  transfers between devices with their start and end apart: 8, of which 4 were waited for; matrix products, arithmetic and copies ran while one was open for 1% of the time, Pallas kernels for 0%

profile of v1, /device:TPU:1, one launch (start us, length us, event | category | flops | bytes accessed | tf_op | source)
XLA Modules:
  0.0 2172.9 jit_solution(5190396444174710127)
XLA Ops:
  7.2 0.0 copy-start
  7.2 0.8 slice_bitcast_fusion.9
  8.0 1.0 convert_element_type.87
  9.0 0.0 copy-start.8
  9.0 0.0 copy-start.7
  9.0 0.0 copy-start.4
  9.1 0.9 add_convert_fusion
  10.0 10.3 all-to-all-start
  20.4 9.8 all-to-all-done
  30.2 0.3 fusion.1
  30.5 0.4 copy.50
  30.9 0.6 fusion.12
  31.5 0.0 copy-start.1
  31.5 0.9 copy-done.1
  32.4 0.6 gather_fusion.1
  33.0 0.1 fusion.49
  33.1 11.3 collective-permute-start.1
  44.4 0.6 gather_fusion
  45.0 0.1 fusion.48
  45.1 1.9 collective-permute-start
  47.0 2.5 reshape.139
  49.5 0.0 copy-start.9
  49.5 1.2 slice.257
  50.7 4.8 collective-permute-done
  55.5 0.7 fusion.47
  56.3 0.2 copy.51
  56.5 0.8 fusion.34
  57.3 0.0 copy-start.3
  57.4 4.6 collective-permute-start.3
  62.0 1.9 collective-permute-start.2
  63.9 1.6 convolution_bitcast_fusion
  65.5 0.6 gather_fusion.3
  66.1 6.4 collective-permute-done.2
  72.4 0.6 gather_fusion.2
  73.0 0.1 select_bitcast_fusion
  73.2 0.2 fusion.45
  73.4 0.8 fusion.30
  74.2 1.0 fusion.53
  75.2 0.0 all-reduce.9.cloned.1.call-update
  75.2 1.1 copy.60
  76.3 0.2 fusion.2
  76.5 0.5 copy.67
  77.0 0.5 broadcast.135
  77.5 2.7 reduce.5
  80.2 0.8 reshape.191
  81.1 7.0 all-to-all-start.1
  88.1 1251.8 %all-reduce.9.cloned.1.call-done = (f32[1024,256]{0,1:T(8,128)}, f32[256,256]{1,0:T(8,128)}) async-done(((f32[1024,256]{0,1:T(8,128)}, f32[256,256]{1,0:T(8,128)}), (f32[1024,256]{0,1:T(8,128)}, f32[256,256]{1,0:T(8,128)})) %all-reduce.9.cloned.1.call-update) | async-done | bytes 1310736 | tf_op jit(solution)/shard_map/psum | solution.py:116
  1339.9 0.0 all-reduce.11.cloned.1.call-update
  1339.9 1.5 convolution_convert_fusion
  1341.4 1.6 reshape.140
  1343.1 0.7 fusion.38
  1343.9 1.3 reshape.192
  1345.2 0.1 copy.63
  1345.2 0.3 copy.59
  1345.5 0.4 convolution_bitcast_fusion.1
  1345.9 0.2 copy.61
  1346.2 617.7 %all-reduce.2 = (f32[1,256]{1,0:T(1,128)S(1)}, f32[9,256]{1,0:T(8,128)S(1)}, f32[16,256]{1,0:T(8,128)S(1)}) all-reduce(f32[1,256]{1,0:T(1,128)S(1)} %bitcast.136, f32[9,256]{1,0:T(8,128)S(1)} %stack.51, f32[16,256]{1,0:T(8,128)S(1)} %reshape.145), channel_id=1, replica_groups=mesh['tm'=4,'pix'=128] {'pix'}, use_global_device_ids=true, to_apply=%region_3.5 | all-reduce | flops 6656 | bytes 53248 | tf_op jit(solution)/shard_map/psum | solution.py:116
  1963.8 197.1 %all-reduce.4 = (f32[1,256]{1,0:T(1,128)S(1)}, f32[9,256]{1,0:T(8,128)S(1)}, f32[16,256]{1,0:T(8,128)S(1)}) all-reduce(f32[1,256]{1,0:T(1,128)S(1)} %get-tuple-element.66, f32[9,256]{1,0:T(8,128)S(1)} %get-tuple-element.67, f32[16,256]{1,0:T(8,128)S(1)} %get-tuple-element.68), channel_id=1, replica_groups=mesh['tm'=4,'pix'=128] {'tm'}, use_global_device_ids=true, to_apply=%region_4.6 | all-reduce | flops 6656 | bytes 53248 | tf_op jit(solution)/shard_map/psum | solution.py:116
  2160.9 0.6 mul.396
  2161.5 0.6 broadcast_multiply_fusion.4
  2162.1 0.6 broadcast_multiply_fusion.3
  2162.7 1.3 broadcast_multiply_fusion
  2164.0 1.3 copy.62
  2165.3 0.7 broadcast_multiply_fusion.1
  (33 shorter events, 0.3 us)
Async XLA Ops:
  7.2 49.3 %copy-start = (bf16[1024,256]{1,0:T(8,128)(2,1)S(1)}, bf16[1024,256]{1,0:T(8,128)(2,1)}, u32[]{:S(2)}) copy-start(bf16[1024,256]{1,0:T(8,128)(2,1)} %param.17) | copy-start | bytes 1572868
  9.0 11.3 copy-start.8
  9.0 11.3 copy-start.7
  9.0 21.2 copy-start.4
  10.0 20.2 all-to-all-start
  20.3 1319.6 %all-reduce.9.cloned.1.call-start = ((), (), s32[]{:S(2)}) async-start(), calls=%async_computation.2 | async-start | bytes 2621440 | tf_op jit(solution)/shard_map/psum | solution.py:116
  31.5 0.9 copy-start.1
  33.1 17.7 collective-permute-start.1
  45.1 10.4 collective-permute-start
  49.5 7.0 copy-start.9
  57.3 8.2 copy-start.3
  57.4 8.1 collective-permute-start.3
  62.0 10.5 collective-permute-start.2
  74.2 1.1 copy-start.2
  81.1 1262.8 %all-to-all-start.1 = ((bf16[4,2,20480]{2,1,0:T(2,128)(2,1)}), bf16[4,2,20480]{2,1,0:T(2,128)(2,1)}, u32[]{:S(2)}, u32[]{:S(2)}) async-start(bf16[4,2,20480]{2,1,0:T(2,128)(2,1)} %reshape.191), calls=%async_computation.1 | async-start | bytes 655360 | tf_op jit(solution)/shard_map/all_to_all | solution.py:59
  88.1 2074.6 %all-reduce.11.cloned.1.call-start = ((), (), s32[]{:S(2)}) async-start(), calls=%async_computation.3 | async-start | bytes 2621440 | tf_op jit(solution)/shard_map/psum | solution.py:116
  1343.8 1.7 copy-start.5
  2164.0 1.3 copy-start.6
Sparse Core Ops, SparseCore 0:
  75.3 1264.5 all-reduce.8
  1343.2 141.6 all-reduce.10
